TPU v7x, 32 devices: a whole 2x2x4 slice. The times are simulated.
32 devices in a mesh: row: 2 (over x), col: 4 (over y, core), layer: 4 (over z).
Axes of the slice: x: 2, y: 2, z: 4, core: 2. Of those that a mesh axis runs over, the one named last changes fastest.
Arguments:
- source_matrix_strip: bfloat16 [4096, 512], P('row', 'col')
- target_matrix_strip: bfloat16 [512, 8192], P('row', ('col', 'layer'))
- stored_tile_flag: int32 [32, 4], P('row', 'col'), may hold values from 0 to 1
- target_place_tile_index: int32 [32, 32], P('row', ('col', 'layer')), may hold values from 0 to 3, as said below
- retained_target_flag: int32 [32, 32], P('row', ('col', 'layer')), may hold values 0 or 1
Outputs:
- clustered: bfloat16 [4096, 4096], P(('row', 'layer'), 'col')
Inputs may be any that keep to these rules, and one draw needn't show every extreme that they name: `target_place_tile_index`: within each block row, the 2 slots of one column tile name distinct column blocks.
All inputs are finite; a program needn't handle non-finite values. No bound on the sum of `retained_target_flag` on one device may be relied on, other than what follows from the above.
Results may differ from a plain program's by a relative error of at most 0.0012.
Values may be sent and summed in bfloat16 or wider, within the bound.
No kernel may reach another device: no remote copies, remote signals or barrier semaphores. Data moves between devices by JAX's collectives and lax.ppermute only.
A program may use at most 64 MiB of HBM per device.

v0:
```python
import jax
import jax.numpy as jnp
from jax import lax
from jax.sharding import PartitionSpec as P

BS = 128
COLB = 4
KOL = 2


def matrix_squaring_step(walk_matrix_result, target_place_tile_index, retained_target_flag):
    block_rows = walk_matrix_result.shape[0] // BS
    product_blocks = walk_matrix_result.reshape(block_rows, BS, COLB, BS)
    block_selector = (
        target_place_tile_index[:, :, None] == jnp.arange(COLB, dtype=jnp.int32)[None, None, :]
    ).astype(jnp.float32)
    picked = jnp.einsum(
        "rsc,rick->rsik", block_selector, product_blocks, precision=lax.Precision.HIGHEST
    )
    retain_weight = retained_target_flag.astype(jnp.float32)
    raised_power_blocks = picked * picked * retain_weight[:, :, None, None]
    row_sums = jnp.sum(raised_power_blocks, axis=2)
    partial_column_sums = jnp.einsum(
        "rsc,rsk->ck", block_selector, row_sums, precision=lax.Precision.HIGHEST
    )
    return (block_selector, raised_power_blocks, partial_column_sums)


def normalize_blocks(block_selector, raised_power_blocks, column_sums, total_rows):
    column_mean = column_sums / jnp.float32(total_rows)
    denominator = (
        jnp.einsum("rsc,ck->rsk", block_selector, column_mean, precision=lax.Precision.HIGHEST)
        + 1e-06
    )
    normalized = (raised_power_blocks / denominator[:, :, None, :]).astype(jnp.bfloat16)
    block_rows = raised_power_blocks.shape[0]
    return jnp.transpose(normalized, (0, 2, 1, 3)).reshape(block_rows * BS, KOL * BS)


def shards(
    source_matrix_strip,
    target_matrix_strip,
    stored_tile_flag,
    target_place_tile_index,
    retained_target_flag,
):
    local_rows = source_matrix_strip.shape[0]
    expanded = jnp.repeat(jnp.repeat(stored_tile_flag, BS, axis=0), BS, axis=1)
    masked = source_matrix_strip * expanded.astype(jnp.bfloat16)
    right_whole = lax.all_gather(target_matrix_strip, "row", axis=0, tiled=True)
    total_rows = local_rows * lax.axis_size("row")
    walk_matrix_result = jnp.dot(
        lax.all_gather(masked, "col", axis=1, tiled=True),
        right_whole,
        preferred_element_type=jnp.float32,
    )
    block_selector, raised_power_blocks, partial_column_sums = matrix_squaring_step(
        walk_matrix_result, target_place_tile_index, retained_target_flag
    )
    column_sums = lax.psum(partial_column_sums, "row")
    arranged = normalize_blocks(block_selector, raised_power_blocks, column_sums, total_rows)
    return lax.all_to_all(arranged, "layer", split_axis=0, concat_axis=1, tiled=True)


def solution(mesh):
    placed = (
        P("row", "col"),
        P("row", ("col", "layer")),
        P("row", "col"),
        P("row", ("col", "layer")),
        P("row", ("col", "layer")),
    )
    return jax.shard_map(
        shards, mesh=mesh, in_specs=placed, out_specs=P(("row", "layer"), "col"), check_vma=False
    )
```

profile of v0, /device:TPU:0, one launch (start us, length us, event | category | flops | bytes accessed | tf_op | source)
XLA Modules:
  0.0 96.9 jit_solution(11177682488823599812)
XLA Ops:
  6.5 0.0 all-gather.2.cloned.1.call-start
  6.5 0.7 convert_bitcast_fusion
  7.2 0.1 broadcast_bitcast_fusion
  7.3 2.2 %broadcast_multiply_fusion = bf16[2048,128]{1,0:T(8,128)(2,1)} fusion(bf16[2048,128]{1,0:T(8,128)(2,1)} %param.5, bf16[2048]{0:T(1024)(128)(2,1)S(1)} %broadcast_bitcast_fusion), kind=kLoop, calls=%fused_computation.5 | loop fusion | flops 262144 | bytes 1052672 | tf_op jit(solution)/shard_map/mul | solution.py:49
  9.4 0.0 all-gather.2.cloned.1.call-update
  9.5 0.7 fusion.2
  10.2 0.1 copy.10
  10.3 0.7 convert_element_type.25
  11.0 0.1 copy.7
  11.0 10.2 %all_gather.7 = bf16[512,512]{1,0:T(8,128)(2,1)S(1)} all-gather(bf16[256,512]{1,0:T(8,128)(2,1)} %param.6), channel_id=1, replica_groups=mesh['row'=2,'col'=4,'layer'=4] {'row'}, dimensions={0}, use_global_device_ids=true | all-gather | bytes 786432 | tf_op jit(solution)/shard_map/all_gather | solution.py:50
  21.2 14.0 %all-gather.2.cloned.1.call-done = bf16[2048,512]{1,0:T(8,128)(2,1)} async-done(((bf16[2048,128]{1,0:T(8,128)(2,1)}), bf16[2048,512]{1,0:T(8,128)(2,1)}) %all-gather.2.cloned.1.call-update) | async-done | bytes 2097168 | tf_op jit(solution)/shard_map/all_gather | solution.py:53
  35.2 4.8 %fusion.10 = f32[2048,512]{1,0:T(8,128)} fusion(bf16[2048,512]{1,0:T(8,128)(2,1)} %all-gather.2.cloned.1.call-done, bf16[512,512]{1,0:T(8,128)(2,1)S(1)} %all_gather.7), kind=kOutput, calls=%fused_computation.18 | convolution fusion | flops 1073741824 | bytes 6815744 | tf_op jit(solution)/shard_map/dot_general | solution.py:52
  39.9 5.2 %reshape.22 = f32[16,128,4,128]{3,2,1,0:T(4,128)} reshape(f32[2048,512]{1,0:T(8,128)} %fusion.10) | data formatting | bytes 8388608 | tf_op jit(solution)/shard_map/reshape | solution.py:13
  45.2 0.0 copy-start
  45.2 7.3 %fusion.9 = (f32[16,2,128]{2,1,0:T(2,128)S(1)}, f32[16,2,128,128]{3,1,2,0:T(2,128)S(1)}) fusion(f32[16,2]{1,0:T(8,128)S(1)} %copy.7, pred[16,2,4,1]{2,1,3,0:T(4,128)(4,1)S(1)} %copy.10, f32[16,128,4,128]{3,2,1,0:T(4,128)} %reshape.22), kind=kOutput, calls=%fused_computation.17 | convolution fusion | flops 26734592 | bytes 6308096 | tf_op jit(solution)/shard_map/rsc,rick->rsik/dot_general | solution.py:17
  52.5 0.0 copy-done
  52.5 0.2 convolution_bitcast_fusion
  52.7 4.9 %psum.7 = f32[4,128]{1,0:T(4,128)S(1)} all-reduce(f32[4,128]{1,0:T(4,128)S(1)} %convolution_bitcast_fusion), channel_id=1, replica_groups=mesh['row'=2,'col'=4,'layer'=4] {'row'}, use_global_device_ids=true, to_apply=%region_1.0 | all-reduce | flops 512 | bytes 4096 | tf_op jit(solution)/shard_map/psum | solution.py:60
  57.6 0.2 convolution_add_fusion
  57.9 0.9 fusion
  58.8 0.7 all_to_all.14
  59.5 29.4 %all_to_all.19 = bf16[4,512,256]{2,1,0:T(8,128)(2,1)S(1)} all-to-all(bf16[4,512,256]{2,1,0:T(8,128)(2,1)S(1)} %all_to_all.14), channel_id=1, replica_groups=mesh['row'=2,'col'=4,'layer'=4] {'layer'}, dimensions={0} | all-to-all | bytes 2097152 | tf_op jit(solution)/shard_map/all_to_all | solution.py:62
  88.9 1.1 %copy.14 = bf16[4,64,8,256]{3,2,0,1:T(8,128)(2,1)} copy(bf16[4,64,8,256]{3,2,1,0:T(8,128)(2,1)S(1)} %bitcast.20) | data formatting | bytes 2097152 | tf_op jit(solution)/shard_map/all_to_all | solution.py:62
  (1 shorter events, 0.0 us)
Async XLA Ops:
  6.5 28.6 %all-gather.2.cloned.1.call-start = ((), (), s32[]{:S(2)}) async-start(), calls=%async_computation.1 | async-start | bytes 2621440 | tf_op jit(solution)/shard_map/all_gather | solution.py:53
  45.2 7.3 %copy-start = (s32[16,2]{0,1:T(2,128)S(1)}, s32[16,2]{0,1:T(2,128)}, u32[]{:S(2)}) copy-start(s32[16,2]{0,1:T(2,128)} %param.8) | copy-start | bytes 388
Sparse Core Ops, SparseCore 0:
  9.6 25.5 all-gather.1
where the time goes:
time: 97.3 us; the launch traced here: 96.9 us
  blocking collectives  44.5 us (46%)
  waiting for transfers between devices  14 us (14%)
  between operations  13.4 us (14%)
  matrix products  12.5 us (13%)
  local copies, waits for them, and re-layouts  7.34 us (8%)
  other arithmetic  5.11 us (5%)
    all_to_all x1, blocking collectives, shards(): lax.all_to_all(arranged, 'layer', split_axis=0, concat_axis=1, tiled=True)  29.4 us
    all_gather x1, waiting for transfers between devices, shards(): lax.all_gather(masked, 'col', axis=1, tiled=True)  14 us
    all_gather x1, blocking collectives, shards(): right_whole = lax.all_gather(target_matrix_strip, 'row', axis=0, tiled=True)  10.2 us
    dot_general x1, matrix products, matrix_squaring_step(): jnp.einsum('rsc,rick->rsik', block_selector, product_blocks, precision=la...  7.34 us
    reshape x1, local copies, waits for them, and re-layouts, matrix_squaring_step(): product_blocks = walk_matrix_result.reshape(block_rows, BS, COLB, BS)  5.23 us
    psum x1, blocking collectives, shards(): column_sums = lax.psum(partial_column_sums, 'row')  4.93 us
    dot_general x1, matrix products, shards(): jnp.dot(lax.all_gather(masked, 'col', axis=1, tiled=True), right_whole, p...  4.76 us
    mul x1, other arithmetic, shards(): masked = source_matrix_strip * expanded.astype(jnp.bfloat16)  2.18 us
  transfers between devices with their start and end apart: 1, of which 1 were waited for; matrix products, arithmetic and copies ran while one was open for 2% of the time, Pallas kernels for 0%

commit v1 on v0

--- a/solution.py
+++ b/solution.py
@@ -6,6 +6,28 @@
 BS = 128
 COLB = 4
 KOL = 2
+
+
+def laid_out(blocks, dim):
+    blocks = jnp.moveaxis(blocks, 0, dim)
+    shape = blocks.shape
+    return blocks.reshape(*shape[:dim], shape[dim] * shape[dim + 1], *shape[dim + 2 :])
+
+
+def ring_gather(array, axis, dim):
+    peers = lax.axis_size(axis)
+    pairs = [(i, (i + 1) % peers) for i in range(peers)]
+    back = [(b, a) for a, b in pairs]
+    lower, upper = ([], [])
+    for lap in range(peers - 1):
+        if lap % 2 == 0:
+            lower.append(lax.ppermute(lower[-1] if lower else array, axis, pairs))
+        else:
+            upper.append(lax.ppermute(upper[-1] if upper else array, axis, back))
+    blocks = jnp.stack([*lower[::-1], array, *upper])
+    shift = lax.axis_index(axis) - len(lower)
+    blocks = blocks[(jnp.arange(peers) - shift) % peers]
+    return laid_out(blocks, dim)
 
 
 def matrix_squaring_step(walk_matrix_result, target_place_tile_index, retained_target_flag):
@@ -50,9 +72,7 @@
     right_whole = lax.all_gather(target_matrix_strip, "row", axis=0, tiled=True)
     total_rows = local_rows * lax.axis_size("row")
     walk_matrix_result = jnp.dot(
-        lax.all_gather(masked, "col", axis=1, tiled=True),
-        right_whole,
-        preferred_element_type=jnp.float32,
+        ring_gather(masked, "col", 1), right_whole, preferred_element_type=jnp.float32
     )
     block_selector, raised_power_blocks, partial_column_sums = matrix_squaring_step(
         walk_matrix_result, target_place_tile_index, retained_target_flag

time: 97.3 us -> 81.5 us (0.84)
  between operations: 13.4 us -> 0.13 us
  waiting for transfers between devices: 14 us -> 6.15 us
  local copies, waits for them, and re-layouts: 7.34 us -> 11.8 us
  starting transfers between devices: 0.01 us -> 4.38 us
  matrix products: 12.5 us -> 8.16 us
    all_gather x1 -> x0, waiting for transfers between devices: 14 us -> none  [shards(): lax.all_gather(masked, 'col', axis=1, tiled=True)]
    dot_general x0 -> x3, local copies, waits for them, and re-layouts: none -> 7.52 us  [shards(): jnp.dot(ring_gather(masked, 'col', 1), right_whole, preferred_element_typ...]
    ppermute x0 -> x3, waiting for transfers between devices: none -> 6.15 us  [the longest x2 6.14 us: ring_gather(): lower.append(lax.ppermute(lower[-1] if lower else array, axis, pairs))]
    reshape x1 -> x0, local copies, waits for them, and re-layouts: 5.23 us -> none  [matrix_squaring_step(): product_blocks = walk_matrix_result.reshape(block_rows, BS, COLB, BS)]
    ppermute x0 -> x3, starting transfers between devices: none -> 4.38 us  [the longest x2 2.36 us: ring_gather(): lower.append(lax.ppermute(lower[-1] if lower else array, axis, pairs))]
    dot_general x1, matrix products: 4.76 us -> 1.25 us  [shards(): jnp.dot(ring_gather(masked, 'col', 1), right_whole, preferred_element_typ...]
    gather x0 -> x1, local copies, waits for them, and re-layouts: none -> 2.16 us  [ring_gather(): blocks = blocks[(jnp.arange(peers) - shift) % peers]]
    another operation x0 -> x2, other arithmetic: none -> 1.79 us  [ring_gather(): blocks = jnp.stack([*lower[::-1], array, *upper])]
  transfers between devices with their start and end apart: 1 -> 3, of which waited for: 1 -> 1; matrix products, arithmetic and copies ran while one was open for 2% -> 2% of each run, Pallas kernels for 0% -> 0%
where the time goes in v1:
time: 81.5 us; the launch traced here: 81.2 us
  blocking collectives  45.1 us (55%)
  local copies, waits for them, and re-layouts  11.8 us (14%)
  matrix products  8.16 us (10%)
  waiting for transfers between devices  6.15 us (8%)
  other arithmetic  5.52 us (7%)
  starting transfers between devices  4.38 us (5%)
    all_to_all x1, blocking collectives, shards(): lax.all_to_all(arranged, 'layer', split_axis=0, concat_axis=1, tiled=True)  30.1 us
    all_gather x1, blocking collectives, shards(): right_whole = lax.all_gather(target_matrix_strip, 'row', axis=0, tiled=True)  9.71 us
    dot_general x3, local copies, waits for them, and re-layouts, shards(): jnp.dot(ring_gather(masked, 'col', 1), right_whole, preferred_element_typ...  7.52 us
    dot_general x1, matrix products, matrix_squaring_step(): jnp.einsum('rsc,rick->rsik', block_selector, product_blocks, precision=la...  6.51 us
    ppermute x2, waiting for transfers between devices, ring_gather(): lower.append(lax.ppermute(lower[-1] if lower else array, axis, pairs))  6.14 us
    psum x1, blocking collectives, shards(): column_sums = lax.psum(partial_column_sums, 'row')  5.28 us
    ppermute x2, starting transfers between devices, ring_gather(): lower.append(lax.ppermute(lower[-1] if lower else array, axis, pairs))  2.36 us
    gather x1, local copies, waits for them, and re-layouts, ring_gather(): blocks = blocks[(jnp.arange(peers) - shift) % peers]  2.16 us
  transfers between devices with their start and end apart: 3, of which 1 were waited for; matrix products, arithmetic and copies ran while one was open for 2% of the time, Pallas kernels for 0%

profile of v1, /device:TPU:0, one launch (start us, length us, event | category | flops | bytes accessed | tf_op | source)
XLA Modules:
  0.0 81.2 jit_solution(6879871850827203873)
XLA Ops:
  0.0 0.0 copy-start
  0.0 0.0 copy-start.2
  0.0 0.7 convert_bitcast_fusion
  0.7 0.1 broadcast_bitcast_fusion
  0.8 1.4 %broadcast_multiply_fusion = bf16[2048,128]{1,0:T(8,128)(2,1)S(1)} fusion(bf16[2048,128]{1,0:T(8,128)(2,1)} %param.5, bf16[2048]{0:T(1024)(128)(2,1)S(1)} %broadcast_bitcast_fusion), kind=kLoop, calls=%fused_computation.11 | loop fusion | flops 262144 | bytes 1052672 | tf_op jit(solution)/shard_map/mul | solution.py:71
  2.2 0.5 collective-permute-start
  2.7 2.0 %collective-permute-start.2 = (bf16[2048,128]{1,0:T(8,128)(2,1)S(1)}, bf16[2048,128]{1,0:T(8,128)(2,1)}, u32[]{:S(2)}, u32[]{:S(2)}) collective-permute-start(bf16[2048,128]{1,0:T(8,128)(2,1)S(1)} %broadcast_multiply_fusion), channel_id=1, source_target_pairs={{4,0},{8,4},{12,8},{0,12},{5,1},{9,5},{13,9},{1,13},{6,2},{10,6},{... | collective-permute-start | bytes 1572872 | tf_op jit(solution)/shard_map/ppermute | solution.py:26
  4.7 9.7 %all_gather.3 = bf16[512,512]{1,0:T(8,128)(2,1)S(1)} all-gather(bf16[256,512]{1,0:T(8,128)(2,1)} %param.6), channel_id=1, replica_groups=mesh['row'=2,'col'=4,'layer'=4] {'row'}, dimensions={0}, use_global_device_ids=true | all-gather | bytes 786432 | tf_op jit(solution)/shard_map/all_gather | solution.py:72
  14.4 0.7 fusion.8
  15.1 0.0 collective-permute-done
  15.1 1.9 %collective-permute-start.1 = (bf16[2048,128]{1,0:T(8,128)(2,1)S(1)}, bf16[2048,128]{1,0:T(8,128)(2,1)}, u32[]{:S(2)}, u32[]{:S(2)}) collective-permute-start(bf16[2048,128]{1,0:T(8,128)(2,1)S(1)} %collective-permute-done), channel_id=1, source_target_pairs={{0,4},{4,8},{8,12},{12,0},{1,5},{5,9},{9,13},{13,1},{2,6},{6,10},{... | collective-permute-start | bytes 1572872 | tf_op jit(solution)/shard_map/ppermute | solution.py:24
  17.0 0.1 reshape.82
  17.1 0.0 copy-done.2
  17.1 0.1 copy.12
  17.2 0.1 copy.18
  17.3 0.0 copy-done
  17.3 0.3 fusion.20
  17.7 0.0 collective-permute-done.2
  17.7 6.1 %collective-permute-done.1 = bf16[2048,128]{1,0:T(8,128)(2,1)} collective-permute-done((bf16[2048,128]{1,0:T(8,128)(2,1)S(1)}, bf16[2048,128]{1,0:T(8,128)(2,1)}, u32[]{:S(2)}, u32[]{:S(2)}) %collective-permute-start.1) | collective-permute-done | bytes 524320 | tf_op jit(solution)/shard_map/ppermute | solution.py:24
  23.8 1.5 %pad_maximum_fusion = bf16[4,2048,128]{2,1,0:T(8,128)(2,1)S(1)} fusion(bf16[1,2048,128]{2,1,0:T(8,128)(2,1)} %bitcast.6, bf16[1,2048,128]{2,1,0:T(8,128)(2,1)S(1)} %fusion.20, bf16[1,2048,128]{2,1,0:T(8,128)(2,1)S(1)} %bitcast.32, bf16[1,2048,128]{2,1,0:T(8,128)(2,1)} %bitcast.3), kind=kLoop, calls=%fused_computation.3 | loop fusion | flops 3145728 | bytes 4194304 | tf_op jit(solution)/shard_map/stack | solution.py:27
  25.3 2.2 %gather_fusion = bf16[4,2048,128]{2,1,0:T(8,128)(2,1)} fusion(bf16[4,2048,128]{2,1,0:T(8,128)(2,1)S(1)} %pad_maximum_fusion, s32[1024]{0:T(1024)S(1)} %pad_clamp_fusion), kind=kCustom, calls=%fused_computation | custom fusion | bytes 4194320 | tf_op jit(solution)/shard_map/gather | solution.py:29
  27.5 4.7 %copy.22 = bf16[2048,4,128]{2,1,0:T(4,128)(2,1)} copy(bf16[2048,4,128]{2,0,1:T(8,128)(2,1)} %bitcast.29) | data formatting | bytes 4194304 | tf_op jit(solution)/shard_map/dot_general | solution.py:74
  32.1 2.7 %reshape.87 = bf16[16,128,512,1]{2,1,3,0:T(8,128)(2,1)S(1)} reshape(bf16[2048,4,128]{2,1,0:T(4,128)(2,1)} %copy.22) | data formatting | bytes 4194304 | tf_op jit(solution)/shard_map/dot_general | solution.py:74
  34.9 1.3 %fusion.5 = f32[16,128,4,128]{3,1,2,0:T(8,128)S(1)} fusion(bf16[16,128,512,1]{2,1,3,0:T(8,128)(2,1)S(1)} %reshape.87, bf16[4,128,512,1]{1,0,2,3:T(4,128)(2,1)S(1)} %reshape.82), kind=kOutput, calls=%fused_computation.9 | convolution fusion | flops 1073741824 | bytes 6815744 | tf_op jit(solution)/shard_map/dot_general | solution.py:74
  36.1 0.0 copy-start.1
  36.1 6.5 %fusion.17 = (f32[16,2,128]{2,1,0:T(2,128)S(1)}, f32[16,2,128,128]{3,1,2,0:T(2,128)S(1)}) fusion(f32[16,2]{1,0:T(8,128)S(1)} %copy.12, pred[16,2,4,1]{2,1,3,0:T(4,128)(4,1)S(1)} %copy.18, f32[16,128,4,128]{3,1,2,0:T(8,128)S(1)} %fusion.5), kind=kOutput, calls=%fused_computation.30 | convolution fusion | flops 26734592 | bytes 6308096 | tf_op jit(solution)/shard_map/rsc,rick->rsik/dot_general | solution.py:39
  42.7 0.0 copy-done.1
  42.7 0.2 convolution_bitcast_fusion
  42.9 5.3 %psum.7 = f32[4,128]{1,0:T(4,128)S(1)} all-reduce(f32[4,128]{1,0:T(4,128)S(1)} %convolution_bitcast_fusion), channel_id=1, replica_groups=mesh['row'=2,'col'=4,'layer'=4] {'row'}, use_global_device_ids=true, to_apply=%region_1.2 | all-reduce | flops 512 | bytes 4096 | tf_op jit(solution)/shard_map/psum | solution.py:80
  48.1 0.2 convolution_add_fusion
  48.4 0.9 %fusion.4 = bf16[16,128,2,128]{3,2,1,0:T(2,128)(2,1)S(1)} fusion(f32[16,2,128,128]{3,1,2,0:T(2,128)S(1)} %get-tuple-element.6, f32[16,2,128]{2,1,0:T(2,128)S(1)} %copy.13), kind=kLoop, calls=%fused_computation.8 | loop fusion | flops 1048576 | bytes 3162112 | tf_op jit(solution)/shard_map/convert_element_type | solution.py:57
  49.3 0.7 all_to_all.14
  50.0 30.1 %all_to_all.19 = bf16[4,512,256]{2,1,0:T(8,128)(2,1)S(1)} all-to-all(bf16[4,512,256]{2,1,0:T(8,128)(2,1)S(1)} %all_to_all.14), channel_id=1, replica_groups=mesh['row'=2,'col'=4,'layer'=4] {'layer'}, dimensions={0} | all-to-all | bytes 2097152 | tf_op jit(solution)/shard_map/all_to_all | solution.py:82
  80.1 1.1 %copy.24 = bf16[4,64,8,256]{3,2,0,1:T(8,128)(2,1)} copy(bf16[4,64,8,256]{3,2,1,0:T(8,128)(2,1)S(1)} %bitcast.30) | data formatting | bytes 2097152 | tf_op jit(solution)/shard_map/all_to_all | solution.py:82
  (4 shorter events, 0.0 us)
Async XLA Ops:
  0.0 17.3 %copy-start = (bf16[2048,128]{1,0:T(8,128)(2,1)S(1)}, bf16[2048,128]{1,0:T(8,128)(2,1)}, u32[]{:S(2)}) copy-start(bf16[2048,128]{1,0:T(8,128)(2,1)} %param.5) | copy-start | bytes 1572868
  0.0 17.1 %copy-start.2 = (s32[16,2]{0,1:T(2,128)S(1)}, s32[16,2]{0,1:T(2,128)}, u32[]{:S(2)}) copy-start(s32[16,2]{0,1:T(2,128)} %param.9) | copy-start | bytes 388
  2.2 12.9 %collective-permute-start = (bf16[2048,128]{1,0:T(8,128)(2,1)S(1)}, bf16[2048,128]{1,0:T(8,128)(2,1)S(1)}, u32[]{:S(2)}, u32[]{:S(2)}) collective-permute-start(bf16[2048,128]{1,0:T(8,128)(2,1)S(1)} %broadcast_multiply_fusion), channel_id=1, source_target_pairs={{0,4},{4,8},{8,12},{12,0},{1,5},{5,9},{9,13},{13,1},{2,6},{6,10},{... | collective-permute-start | bytes 1572872 | tf_op jit(solution)/shard_map/ppermute | solution.py:24
  2.7 15.0 %collective-permute-start.2 = (bf16[2048,128]{1,0:T(8,128)(2,1)S(1)}, bf16[2048,128]{1,0:T(8,128)(2,1)}, u32[]{:S(2)}, u32[]{:S(2)}) collective-permute-start(bf16[2048,128]{1,0:T(8,128)(2,1)S(1)} %broadcast_multiply_fusion), channel_id=1, source_target_pairs={{4,0},{8,4},{12,8},{0,12},{5,1},{9,5},{13,9},{1,13},{6,2},{10,6},{... | collective-permute-start | bytes 1572872 | tf_op jit(solution)/shard_map/ppermute | solution.py:26
  15.1 8.7 %collective-permute-start.1 = (bf16[2048,128]{1,0:T(8,128)(2,1)S(1)}, bf16[2048,128]{1,0:T(8,128)(2,1)}, u32[]{:S(2)}, u32[]{:S(2)}) collective-permute-start(bf16[2048,128]{1,0:T(8,128)(2,1)S(1)} %collective-permute-done), channel_id=1, source_target_pairs={{0,4},{4,8},{8,12},{12,0},{1,5},{5,9},{9,13},{13,1},{2,6},{6,10},{... | collective-permute-start | bytes 1572872 | tf_op jit(solution)/shard_map/ppermute | solution.py:24
  36.1 6.5 %copy-start.1 = (s32[16,2]{0,1:T(2,128)S(1)}, s32[16,2]{0,1:T(2,128)}, u32[]{:S(2)}) copy-start(s32[16,2]{0,1:T(2,128)} %param.8) | copy-start | bytes 388
